TPU v7x, 32 devices: a whole 2x2x4 slice. The times are simulated.
32 devices in a mesh: rows: 4 (over y, core), feat: 8 (over z, x).
Axes of the slice: x: 2, y: 2, z: 4, core: 2. Of those that a mesh axis runs over, the one named last changes fastest.
Arguments:
- margins: float32 [12288, 32], P(('rows', 'feat')), may hold values from -30 to 260
- labels: int32 [12288], P(('rows', 'feat')), may hold values from 0 to 31
- row_bins: int32 [1024, 12288], P('feat', 'rows'), may hold values from 0 to 63
- parents: int32 [12288], P('rows'), may hold values from 0 to 7
- split_feature: int32 [8], replicated, may hold values from 0 to 1023
- split_bin: int32 [8], replicated, may hold values from 16 to 47
- leaf_values: float32 [16, 32], replicated, may hold values from -4 to 4
Outputs:
- split_gains: float32 [16, 1024, 64], P('rows', 'feat')
- node_totals: float32 [16, 64], replicated
All inputs are finite; a program needn't handle non-finite values.
Results may differ from a plain program's by a relative error of at most 0.0017.
Values may be sent and summed in bfloat16 or wider, within the bound.
No kernel may reach another device: no remote copies, remote signals or barrier semaphores. Data moves between devices by JAX's collectives and lax.ppermute only.
A program may use at most 192 MiB of HBM per device.

v0:
```python
import jax
import jax.numpy as jnp
from jax import lax
from jax.sharding import PartitionSpec as P

BINS = 64
hess_ridge = 1.0


def prefix(value, axis, join, neutral):
    count, mine = (lax.axis_size(axis), lax.axis_index(axis))
    pieces = lax.all_gather(value, axis)
    subtotal = jnp.full_like(value, 0) + jnp.asarray(neutral, value.dtype)

    def turn(position, subtotal):
        longer = join(subtotal, pieces[position])
        return jnp.where(position < mine, longer, subtotal)

    return lax.fori_loop(0, count - 1, turn, subtotal)


def gain_scores(left_sums, totals, classes):
    grad_left = left_sums[..., :classes]
    hess_left = left_sums[..., classes:]
    grad_whole = totals[..., :classes]
    hess_whole = totals[..., classes:]
    grad_right = grad_whole - grad_left
    hess_right = hess_whole - hess_left
    score = (
        grad_left * grad_left / (hess_left + hess_ridge)
        + grad_right * grad_right / (hess_right + hess_ridge)
        - grad_whole * grad_whole / (hess_whole + hess_ridge)
    )
    return jnp.mean(score, axis=-1)


def add_terms(earlier, later):
    return earlier + later


def body(margins, labels, row_bins, parents, split_feature, split_bin, leaf_values):
    feat_dev, group_rows = row_bins.shape
    classes = margins.shape[1]
    node_count = leaf_values.shape[0]
    parent_count = split_feature.shape[0]
    bin_count = BINS
    feat_size = lax.axis_size("feat")
    feat_index = lax.axis_index("feat")
    own_rows = group_rows // feat_size
    parent_hot = parents[:, None] == jnp.arange(parent_count, dtype=jnp.int32)[None, :]
    row_feature = jnp.sum(jnp.where(parent_hot, split_feature[None, :], 0), axis=1)
    row_threshold = jnp.sum(jnp.where(parent_hot, split_bin[None, :], 0), axis=1)
    local_column = row_feature - feat_index * feat_dev
    column_hot = local_column[None, :] == jnp.arange(feat_dev, dtype=jnp.int32)[:, None]
    is_owned = jnp.any(column_hot, axis=0)
    chosen = jnp.sum(jnp.where(column_hot, row_bins, 0), axis=0)
    right_part = jnp.where(is_owned & (chosen > row_threshold), 1.0, 0.0).astype(jnp.float32)
    right_all = lax.psum(right_part.astype(jnp.bfloat16), "feat").astype(jnp.float32)
    node_all = 2 * parents + (right_all > 0.5).astype(jnp.int32)
    node_own = lax.dynamic_slice_in_dim(node_all, feat_index * own_rows, own_rows)
    node_hot_own = (node_own[:, None] == jnp.arange(node_count, dtype=jnp.int32)[None, :]).astype(
        jnp.float32
    )
    logits = margins + jnp.dot(node_hot_own, leaf_values, precision=lax.Precision.HIGHEST)
    probabilities = jax.nn.softmax(logits, axis=1)
    label_hot = (labels[:, None] == jnp.arange(classes, dtype=jnp.int32)[None, :]).astype(
        jnp.float32
    )
    gradient = probabilities - label_hot
    hessian = 2.0 * probabilities * (1.0 - probabilities)
    grad_hess = jnp.concatenate([gradient, hessian], axis=1).astype(jnp.bfloat16)
    partial_totals = lax.dot_general(
        node_hot_own.astype(jnp.bfloat16),
        grad_hess,
        (((0,), (0,)), ((), ())),
        preferred_element_type=jnp.float32,
    )
    node_totals = lax.psum(partial_totals, ("rows", "feat"))
    grad_all = lax.all_gather(grad_hess, "feat", axis=0, tiled=True)
    row_size = lax.axis_size("rows")
    node_hot = node_all[:, None] == jnp.arange(node_count, dtype=jnp.int32)[None, :]
    weighted = jnp.where(node_hot[:, :, None], grad_all[:, None, :], jnp.zeros((), jnp.bfloat16))
    flat_weighted = weighted.reshape(group_rows, node_count * 2 * classes)
    own_bins = bin_count // row_size
    span_rows = own_bins * feat_dev * lax.axis_size("rows")
    bin_span = span_rows // feat_dev
    bin_group = 8

    def one_group(offset):
        values = offset + jnp.arange(bin_group, dtype=jnp.int32)
        one_hot = (row_bins[None, :, :] == values[:, None, None]).astype(jnp.bfloat16)
        one_hot = one_hot.reshape(bin_group * feat_dev, group_rows)
        return jnp.dot(one_hot, flat_weighted, preferred_element_type=jnp.float32)

    blocks = lax.map(one_group, jnp.arange(0, bin_span, bin_group, dtype=jnp.int32))
    own_hist = lax.psum_scatter(
        blocks.reshape(span_rows, node_count * 2 * classes), "rows", scatter_dimension=0, tiled=True
    )
    shaped = own_hist.reshape(own_bins, feat_dev, node_count, 2 * classes)
    running = jnp.cumsum(shaped, axis=0)
    before = prefix(running[-1], "rows", add_terms, jnp.zeros_like(running[-1]))
    left_sums = running + before[None]
    gains_here = gain_scores(left_sums, node_totals[None, None], classes)
    gains_moved = jnp.transpose(gains_here, (2, 1, 0))
    split_gains = lax.all_to_all(gains_moved, "rows", split_axis=0, concat_axis=2, tiled=True)
    return (split_gains, node_totals)


def solution(mesh):
    return jax.shard_map(
        body,
        mesh=mesh,
        in_specs=(
            P(("rows", "feat"), None),
            P(("rows", "feat")),
            P("feat", "rows"),
            P("rows"),
            P(),
            P(),
            P(),
        ),
        out_specs=(P("rows", "feat", None), P()),
        check_vma=False,
    )
```

profile of v0, /device:TPU:0, one launch (start us, length us, event | category | flops | bytes accessed | tf_op | source)
XLA Modules:
  0.0 532.2 jit_solution(12949149705158159860)
XLA Ops:
  7.3 0.8 select_reduce_fusion.1
  8.3 1.6 select_reduce_fusion
  9.9 23.4 %psum.14 = bf16[3072]{0:T(1024)(128)(2,1)S(1)} all-reduce(bf16[3072]{0:T(1024)(128)(2,1)S(1)} %select_convert_fusion), channel_id=1, replica_groups=mesh['rows'=4,'feat'=8] {'feat'}, use_global_device_ids=true, to_apply=%region_4.5 | all-reduce | flops 3072 | bytes 12288 | tf_op jit(solution)/shard_map/psum | solution.py:58
  33.3 0.7 convert_add_fusion
  34.2 1.1 fusion.10
  35.3 0.7 subtract_convert_fusion
  36.1 31.2 %all_gather.6 = bf16[3072,64]{0,1:T(8,128)(2,1)S(1)} all-gather(bf16[384,64]{0,1:T(8,128)(2,1)S(1)} %pad_maximum_fusion), channel_id=1, replica_groups=mesh['rows'=4,'feat'=8] {'feat'}, dimensions={0}, use_global_device_ids=true | all-gather | bytes 442368 | tf_op jit(solution)/shard_map/all_gather | solution.py:79
  67.2 108.7 %while.25 = (s32[]{:T(128)}, f32[8,1024,1024]{2,1,0:T(8,128)}, s32[128,3072]{1,0:T(8,128)}, s32[8]{0:T(128)S(1)}, bf16[3072,64]{0,1:T(8,128)(2,1)S(1)}, /*index=5*/pred[3072,16]{0,1:T(8,128)(4,1)S(1)}, s32[]{:T(128)}) while((s32[]{:T(128)}, f32[8,1024,1024]{2,1,0:T(8,128)}, s32[128,3072]{1,0:T(8,128)}, s32[8]{0:T(128)S(1)}, ...), condition=%wide.region_8.9_spmd.clone, body=%wide.region_7.8_spmd.clone.sunk | while | flops 6448742400 | bytes 25092764 | solution.py:95
  67.2 0.6 dynamic_slice.20
  67.8 0.6 iota_add_fusion.2
  68.5 3.4 bitcast_compare_fusion.2
  71.9 0.6 broadcast_select_fusion.2
  72.5 8.3 %bitcast_dynamic-update-slice_fusion.2 = f32[8,1024,1024]{2,1,0:T(8,128)} fusion(f32[8,1024,1024]{2,1,0:T(8,128)} %get-tuple-element.270, s32[]{:T(128)} %get-tuple-element.269, pred[1024,3072]{1,0:T(32,128)(4,1)S(1)} %bitcast_compare_fusion.2, bf16[3072,1024]{0,1:T(8,128)(2,1)S(1)} %bitcast.48), kind=kOutput, calls=%fused_computation.3.clone.1 | convolution fusion | flops 6442450944 | bytes 13632000 | tf_op jit(solution)/shard_map/while/body/eval_jaxpr/dot_general | solution.py:93
  80.9 0.6 dynamic_slice.20
  81.4 0.6 iota_add_fusion.2
  82.2 3.4 bitcast_compare_fusion.2
  85.6 0.6 broadcast_select_fusion.2
  86.2 8.3 %bitcast_dynamic-update-slice_fusion.2 = f32[8,1024,1024]{2,1,0:T(8,128)} fusion(f32[8,1024,1024]{2,1,0:T(8,128)} %get-tuple-element.270, s32[]{:T(128)} %get-tuple-element.269, pred[1024,3072]{1,0:T(32,128)(4,1)S(1)} %bitcast_compare_fusion.2, bf16[3072,1024]{0,1:T(8,128)(2,1)S(1)} %bitcast.48), kind=kOutput, calls=%fused_computation.3.clone.1 | convolution fusion | flops 6442450944 | bytes 13632000 | tf_op jit(solution)/shard_map/while/body/eval_jaxpr/dot_general | solution.py:93
  94.5 0.6 dynamic_slice.20
  95.0 0.6 iota_add_fusion.2
  95.8 3.4 bitcast_compare_fusion.2
  99.2 0.6 broadcast_select_fusion.2
  99.7 8.3 %bitcast_dynamic-update-slice_fusion.2 = f32[8,1024,1024]{2,1,0:T(8,128)} fusion(f32[8,1024,1024]{2,1,0:T(8,128)} %get-tuple-element.270, s32[]{:T(128)} %get-tuple-element.269, pred[1024,3072]{1,0:T(32,128)(4,1)S(1)} %bitcast_compare_fusion.2, bf16[3072,1024]{0,1:T(8,128)(2,1)S(1)} %bitcast.48), kind=kOutput, calls=%fused_computation.3.clone.1 | convolution fusion | flops 6442450944 | bytes 13632000 | tf_op jit(solution)/shard_map/while/body/eval_jaxpr/dot_general | solution.py:93
  108.0 0.6 dynamic_slice.20
  108.6 0.6 iota_add_fusion.2
  109.3 3.4 bitcast_compare_fusion.2
  112.7 0.6 broadcast_select_fusion.2
  113.3 8.3 %bitcast_dynamic-update-slice_fusion.2 = f32[8,1024,1024]{2,1,0:T(8,128)} fusion(f32[8,1024,1024]{2,1,0:T(8,128)} %get-tuple-element.270, s32[]{:T(128)} %get-tuple-element.269, pred[1024,3072]{1,0:T(32,128)(4,1)S(1)} %bitcast_compare_fusion.2, bf16[3072,1024]{0,1:T(8,128)(2,1)S(1)} %bitcast.48), kind=kOutput, calls=%fused_computation.3.clone.1 | convolution fusion | flops 6442450944 | bytes 13632000 | tf_op jit(solution)/shard_map/while/body/eval_jaxpr/dot_general | solution.py:93
  121.6 0.6 dynamic_slice.20
  122.2 0.6 iota_add_fusion.2
  122.9 3.4 bitcast_compare_fusion.2
  126.3 0.6 broadcast_select_fusion.2
  126.9 8.3 %bitcast_dynamic-update-slice_fusion.2 = f32[8,1024,1024]{2,1,0:T(8,128)} fusion(f32[8,1024,1024]{2,1,0:T(8,128)} %get-tuple-element.270, s32[]{:T(128)} %get-tuple-element.269, pred[1024,3072]{1,0:T(32,128)(4,1)S(1)} %bitcast_compare_fusion.2, bf16[3072,1024]{0,1:T(8,128)(2,1)S(1)} %bitcast.48), kind=kOutput, calls=%fused_computation.3.clone.1 | convolution fusion | flops 6442450944 | bytes 13632000 | tf_op jit(solution)/shard_map/while/body/eval_jaxpr/dot_general | solution.py:93
  135.2 0.6 dynamic_slice.20
  135.8 0.6 iota_add_fusion.2
  136.5 3.4 bitcast_compare_fusion.2
  139.9 0.6 broadcast_select_fusion.2
  140.5 8.3 %bitcast_dynamic-update-slice_fusion.2 = f32[8,1024,1024]{2,1,0:T(8,128)} fusion(f32[8,1024,1024]{2,1,0:T(8,128)} %get-tuple-element.270, s32[]{:T(128)} %get-tuple-element.269, pred[1024,3072]{1,0:T(32,128)(4,1)S(1)} %bitcast_compare_fusion.2, bf16[3072,1024]{0,1:T(8,128)(2,1)S(1)} %bitcast.48), kind=kOutput, calls=%fused_computation.3.clone.1 | convolution fusion | flops 6442450944 | bytes 13632000 | tf_op jit(solution)/shard_map/while/body/eval_jaxpr/dot_general | solution.py:93
  148.8 0.6 dynamic_slice.20
  149.4 0.6 iota_add_fusion.2
  150.1 3.4 bitcast_compare_fusion.2
  153.5 0.6 broadcast_select_fusion.2
  154.1 8.3 %bitcast_dynamic-update-slice_fusion.2 = f32[8,1024,1024]{2,1,0:T(8,128)} fusion(f32[8,1024,1024]{2,1,0:T(8,128)} %get-tuple-element.270, s32[]{:T(128)} %get-tuple-element.269, pred[1024,3072]{1,0:T(32,128)(4,1)S(1)} %bitcast_compare_fusion.2, bf16[3072,1024]{0,1:T(8,128)(2,1)S(1)} %bitcast.48), kind=kOutput, calls=%fused_computation.3.clone.1 | convolution fusion | flops 6442450944 | bytes 13632000 | tf_op jit(solution)/shard_map/while/body/eval_jaxpr/dot_general | solution.py:93
  162.4 0.6 dynamic_slice.20
  162.9 0.6 iota_add_fusion.2
  163.7 3.4 bitcast_compare_fusion.2
  167.1 0.6 broadcast_select_fusion.2
  167.6 8.3 %bitcast_dynamic-update-slice_fusion.2 = f32[8,1024,1024]{2,1,0:T(8,128)} fusion(f32[8,1024,1024]{2,1,0:T(8,128)} %get-tuple-element.270, s32[]{:T(128)} %get-tuple-element.269, pred[1024,3072]{1,0:T(32,128)(4,1)S(1)} %bitcast_compare_fusion.2, bf16[3072,1024]{0,1:T(8,128)(2,1)S(1)} %bitcast.48), kind=kOutput, calls=%fused_computation.3.clone.1 | convolution fusion | flops 6442450944 | bytes 13632000 | tf_op jit(solution)/shard_map/while/body/eval_jaxpr/dot_general | solution.py:93
  175.9 31.1 %copy.51 = f32[8192,1024]{0,1:T(8,128)} copy(f32[8192,1024]{1,0:T(8,128)} %bitcast.49) | data formatting | bytes 67108864 | tf_op jit(solution)/shard_map/reshape | solution.py:97
  207.3 229.4 %reduce-scatter.2.cloned.1.call-done = f32[2048,1024]{0,1:T(8,128)} async-done(((f32[8192,1024]{0,1:T(8,128)}), f32[2048,1024]{0,1:T(8,128)}) %reduce-scatter.2.cloned.1.call-update) | async-done | bytes 8388624 | tf_op jit(solution)/shard_map/reduce_scatter | solution.py:96
  436.7 8.6 %copy.62 = f32[128,8,16,128]{3,2,1,0:T(8,128)} copy(f32[128,8,16,128]{3,1,2,0:T(8,128)} %bitcast.51) | data formatting | bytes 16777216
  445.3 15.0 %fusion.2 = f32[16,128,16,64]{1,2,3,0:T(8,128)} fusion(f32[16,128,16,64]{1,0,3,2:T(8,128)} %bitcast.50), kind=kOutput, calls=%fused_computation.8 | output fusion | flops 31457280 | bytes 16777216 | tf_op jit(solution)/shard_map/jit(cumsum)/reduce_window_sum | solution.py:100
  460.3 1.1 slice.20
  461.4 1.0 copy.53
  462.7 39.9 %psum.15 = f32[16,64]{1,0:T(8,128)S(1)} all-reduce(f32[16,64]{1,0:T(8,128)S(1)} %fusion.5), channel_id=1, replica_groups=mesh['rows'=4,'feat'=8] {'rows','feat'}, use_global_device_ids=true, to_apply=%region_13.14 | all-reduce | flops 1024 | bytes 8192 | tf_op jit(solution)/shard_map/psum | solution.py:78
  503.2 5.8 %while.26 = (s32[]{:T(128)}, f32[128,16,64]{2,1,0:T(8,128)S(1)}, s32[]{:T(128)}, f32[4,128,16,64]{1,3,2,0:T(8,128)}, s32[]{:T(128)}, /*index=5*/s32[]{:T(128)}) while((s32[]{:T(128)}, f32[128,16,64]{2,1,0:T(8,128)S(1)}, s32[]{:T(128)}, f32[4,128,16,64]{1,3,2,0:T(8,128)}, s32[]{:T(128)}, /*index=5*/s32[]{:T(128)}) %tuple.67), condition=%wide.region_12.13_spmd.clone, body=%wide.region_11.12_spmd.clone.sunk | while | flops 393220 | bytes 3670109 | solution.py:19
  503.2 1.1 constant_dynamic-slice_fusion.2
  505.1 1.1 constant_dynamic-slice_fusion.2
  507.0 1.1 constant_dynamic-slice_fusion.2
  508.9 0.6 copy.55
  509.5 4.4 broadcast_add_fusion
  513.9 2.7 subtract_reduce_fusion
  516.7 8.0 %all_to_all.18 = f32[16,128,16]{1,2,0:T(8,128)S(1)} all-to-all(f32[16,128,16]{1,2,0:T(8,128)S(1)} %copy.59), channel_id=1, replica_groups=mesh['rows'=4,'feat'=8] {'rows'}, dimensions={0} | all-to-all | bytes 262144 | tf_op jit(solution)/shard_map/all_to_all | solution.py:105
  524.7 0.7 copy.60
  (42 shorter events, 4.6 us)
Async XLA Ops:
  7.2 27.0 %copy-start = (f32[16,32]{1,0:T(8,128)S(1)}, f32[16,32]{1,0:T(8,128)}, u32[]{:S(2)}) copy-start(f32[16,32]{1,0:T(8,128)} %param.17) | copy-start | bytes 6148
  7.2 429.5 %reduce-scatter.2.cloned.1.call-start = ((), (), s32[]{:S(2)}) async-start(), calls=%async_computation.2 | async-start | bytes 41943040 | tf_op jit(solution)/shard_map/reduce_scatter | solution.py:96
  207.1 295.8 %all-gather.2.cloned.1.call-start = ((), (), s32[]{:S(2)}) async-start(), calls=%async_computation.3 | async-start | bytes 2621440 | tf_op jit(solution)/shard_map/all_gather | solution.py:12
  502.6 0.6 copy-start.2
  509.5 15.9 %copy-start.1 = (f32[16,32]{1,0:T(8,128)S(1)}, f32[16,32]{1,0:T(8,128)}, u32[]{:S(2)}) copy-start(f32[16,32]{1,0:T(8,128)} %param.17) | copy-start | bytes 6148
Sparse Core Ops, SparseCore 0:
  207.2 229.4 reduce-scatter.1
  462.5 22.7 all-gather.1
where the time goes:
time: 534 us; the launch traced here: 532 us
  waiting for transfers between devices  229 us (43%)
  blocking collectives  102 us (19%)
  matrix products  67.8 us (13%)
  other arithmetic  64.3 us (12%)
  local copies, waits for them, and re-layouts  53.6 us (10%)
  between operations  14.2 us (3%)
    reduce_scatter x1, waiting for transfers between devices, body(): lax.psum_scatter(blocks.reshape(span_rows, node_count * 2 * classes), 'ro...  229 us
    dot_general x8, matrix products, one_group(): return jnp.dot(one_hot, flat_weighted, preferred_element_type=jnp.float32)  66.4 us
    psum x1, blocking collectives, body(): node_totals = lax.psum(partial_totals, ('rows', 'feat'))  39.9 us
    all_gather x1, blocking collectives, body(): grad_all = lax.all_gather(grad_hess, 'feat', axis=0, tiled=True)  31.2 us
    reshape x1, local copies, waits for them, and re-layouts, body(): blocks.reshape(span_rows, node_count * 2 * classes)  31.1 us
    eq x8, other arithmetic, one_group(): row_bins[None, :, :] == values[:, None, None]  27.1 us
    psum x1, blocking collectives, body(): lax.psum(right_part.astype(jnp.bfloat16), 'feat').astype(jnp.float32)  23.4 us
    another operation x1, other arithmetic, body(): running = jnp.cumsum(shaped, axis=0)  15 us
  transfers between devices with their start and end apart: 2, of which 1 were waited for; matrix products, arithmetic and copies ran while one was open for 0% of the time, Pallas kernels for 0%

commit v1 on v0

--- a/solution.py
+++ b/solution.py
@@ -5,6 +5,18 @@
 
 BINS = 64
 hess_ridge = 1.0
+
+
+def doubled_up(value, axis, dim):
+    ways, here = (lax.axis_size(axis), lax.axis_index(axis))
+    grown, reach = (value, 1)
+    while reach < ways:
+        theirs = lax.ppermute(grown, axis, [(d, d ^ reach) for d in range(ways)])
+        mine_first = jnp.concatenate([grown, theirs], axis=dim)
+        theirs_first = jnp.concatenate([theirs, grown], axis=dim)
+        grown = jnp.where(here & reach == 0, mine_first, theirs_first)
+        reach = 2 * reach
+    return grown
 
 
 def prefix(value, axis, join, neutral):
@@ -76,7 +88,7 @@
         preferred_element_type=jnp.float32,
     )
     node_totals = lax.psum(partial_totals, ("rows", "feat"))
-    grad_all = lax.all_gather(grad_hess, "feat", axis=0, tiled=True)
+    grad_all = doubled_up(grad_hess, "feat", 0)
     row_size = lax.axis_size("rows")
     node_hot = node_all[:, None] == jnp.arange(node_count, dtype=jnp.int32)[None, :]
     weighted = jnp.where(node_hot[:, :, None], grad_all[:, None, :], jnp.zeros((), jnp.bfloat16))

time: 534 us -> 521 us (0.976)
  blocking collectives: 102 us -> 71.2 us
  waiting for transfers between devices: 229 us -> 248 us
    all_gather x1 -> x0, blocking collectives: 31.2 us -> none  [body(): grad_all = lax.all_gather(grad_hess, 'feat', axis=0, tiled=True)]
    ppermute x0 -> x3, waiting for transfers between devices: none -> 18.3 us  [doubled_up(): theirs = lax.ppermute(grown, axis, [(d, d ^ reach) for d in range(ways)])]
  transfers between devices with their start and end apart: 2 -> 5, of which waited for: 1 -> 4; matrix products, arithmetic and copies ran while one was open for 0% -> 0% of each run, Pallas kernels for 0% -> 0%
where the time goes in v1:
time: 521 us; the launch traced here: 520 us
  waiting for transfers between devices  248 us (48%)
  blocking collectives  71.2 us (14%)
  matrix products  67.8 us (13%)
  other arithmetic  64.4 us (12%)
  local copies, waits for them, and re-layouts  53.6 us (10%)
  between operations  14.2 us (3%)
    reduce_scatter x1, waiting for transfers between devices, body(): lax.psum_scatter(blocks.reshape(span_rows, node_count * 2 * classes), 'ro...  229 us
    dot_general x8, matrix products, one_group(): return jnp.dot(one_hot, flat_weighted, preferred_element_type=jnp.float32)  66.4 us
    psum x1, blocking collectives, body(): node_totals = lax.psum(partial_totals, ('rows', 'feat'))  39.9 us
    reshape x1, local copies, waits for them, and re-layouts, body(): blocks.reshape(span_rows, node_count * 2 * classes)  31.1 us
    eq x8, other arithmetic, one_group(): row_bins[None, :, :] == values[:, None, None]  27.1 us
    psum x1, blocking collectives, body(): lax.psum(right_part.astype(jnp.bfloat16), 'feat').astype(jnp.float32)  23.4 us
    ppermute x3, waiting for transfers between devices, doubled_up(): theirs = lax.ppermute(grown, axis, [(d, d ^ reach) for d in range(ways)])  18.3 us
    another operation x1, other arithmetic, body(): running = jnp.cumsum(shaped, axis=0)  15 us
  transfers between devices with their start and end apart: 5, of which 4 were waited for; matrix products, arithmetic and copies ran while one was open for 0% of the time, Pallas kernels for 0%

profile of v1, /device:TPU:0, one launch (start us, length us, event | category | flops | bytes accessed | tf_op | source)
XLA Modules:
  0.0 519.7 jit_solution(10273535343297673320)
XLA Ops:
  7.2 0.8 select_reduce_fusion.1
  8.3 1.6 select_reduce_fusion
  9.9 23.4 %psum.14 = bf16[3072]{0:T(1024)(128)(2,1)S(1)} all-reduce(bf16[3072]{0:T(1024)(128)(2,1)S(1)} %select_convert_fusion), channel_id=1, replica_groups=mesh['rows'=4,'feat'=8] {'feat'}, use_global_device_ids=true, to_apply=%region_4.5 | all-reduce | flops 3072 | bytes 12288 | tf_op jit(solution)/shard_map/psum | solution.py:70
  33.3 0.7 convert_add_fusion
  34.1 1.1 fusion.10
  35.3 0.7 subtract_convert_fusion
  36.1 4.1 collective-permute-done
  40.3 6.6 %collective-permute-done.1 = bf16[768,64]{0,1:T(8,128)(2,1)S(1)} collective-permute-done((bf16[768,64]{0,1:T(8,128)(2,1)S(1)}, bf16[768,64]{0,1:T(8,128)(2,1)S(1)}, u32[]{:S(2)}, u32[]{:S(2)}) %collective-permute-start.1) | collective-permute-done | bytes 98336 | tf_op jit(solution)/shard_map/ppermute | solution.py:14
  47.1 7.6 %collective-permute-done.2 = bf16[1536,64]{0,1:T(8,128)(2,1)S(1)} collective-permute-done((bf16[1536,64]{0,1:T(8,128)(2,1)S(1)}, bf16[1536,64]{0,1:T(8,128)(2,1)S(1)}, u32[]{:S(2)}, u32[]{:S(2)}) %collective-permute-start.2) | collective-permute-done | bytes 196640 | tf_op jit(solution)/shard_map/ppermute | solution.py:14
  54.8 108.7 %while.25 = (s32[]{:T(128)}, f32[8,1024,1024]{2,1,0:T(8,128)}, s32[128,3072]{1,0:T(8,128)}, s32[8]{0:T(128)S(1)}, bf16[3072,64]{0,1:T(8,128)(2,1)S(1)}, /*index=5*/pred[3072,16]{0,1:T(8,128)(4,1)S(1)}, s32[]{:T(128)}) while((s32[]{:T(128)}, f32[8,1024,1024]{2,1,0:T(8,128)}, s32[128,3072]{1,0:T(8,128)}, s32[8]{0:T(128)S(1)}, ...), condition=%wide.region_8.9_spmd.clone, body=%wide.region_7.8_spmd.clone.sunk | while | flops 6448742400 | bytes 25092764 | solution.py:107
  54.8 0.6 dynamic_slice.20
  55.4 0.6 iota_add_fusion.2
  56.1 3.4 bitcast_compare_fusion.2
  59.5 0.6 broadcast_select_fusion.2
  60.1 8.3 %bitcast_dynamic-update-slice_fusion.2 = f32[8,1024,1024]{2,1,0:T(8,128)} fusion(f32[8,1024,1024]{2,1,0:T(8,128)} %get-tuple-element.270, s32[]{:T(128)} %get-tuple-element.269, pred[1024,3072]{1,0:T(32,128)(4,1)S(1)} %bitcast_compare_fusion.2, bf16[3072,1024]{0,1:T(8,128)(2,1)S(1)} %bitcast.48), kind=kOutput, calls=%fused_computation.3.clone.1 | convolution fusion | flops 6442450944 | bytes 13632000 | tf_op jit(solution)/shard_map/while/body/eval_jaxpr/dot_general | solution.py:105
  68.4 0.6 dynamic_slice.20
  69.0 0.6 iota_add_fusion.2
  69.7 3.4 bitcast_compare_fusion.2
  73.1 0.6 broadcast_select_fusion.2
  73.7 8.3 %bitcast_dynamic-update-slice_fusion.2 = f32[8,1024,1024]{2,1,0:T(8,128)} fusion(f32[8,1024,1024]{2,1,0:T(8,128)} %get-tuple-element.270, s32[]{:T(128)} %get-tuple-element.269, pred[1024,3072]{1,0:T(32,128)(4,1)S(1)} %bitcast_compare_fusion.2, bf16[3072,1024]{0,1:T(8,128)(2,1)S(1)} %bitcast.48), kind=kOutput, calls=%fused_computation.3.clone.1 | convolution fusion | flops 6442450944 | bytes 13632000 | tf_op jit(solution)/shard_map/while/body/eval_jaxpr/dot_general | solution.py:105
  82.0 0.6 dynamic_slice.20
  82.6 0.6 iota_add_fusion.2
  83.3 3.4 bitcast_compare_fusion.2
  86.7 0.6 broadcast_select_fusion.2
  87.3 8.3 %bitcast_dynamic-update-slice_fusion.2 = f32[8,1024,1024]{2,1,0:T(8,128)} fusion(f32[8,1024,1024]{2,1,0:T(8,128)} %get-tuple-element.270, s32[]{:T(128)} %get-tuple-element.269, pred[1024,3072]{1,0:T(32,128)(4,1)S(1)} %bitcast_compare_fusion.2, bf16[3072,1024]{0,1:T(8,128)(2,1)S(1)} %bitcast.48), kind=kOutput, calls=%fused_computation.3.clone.1 | convolution fusion | flops 6442450944 | bytes 13632000 | tf_op jit(solution)/shard_map/while/body/eval_jaxpr/dot_general | solution.py:105
  95.6 0.6 dynamic_slice.20
  96.2 0.6 iota_add_fusion.2
  96.9 3.4 bitcast_compare_fusion.2
  100.3 0.6 broadcast_select_fusion.2
  100.9 8.3 %bitcast_dynamic-update-slice_fusion.2 = f32[8,1024,1024]{2,1,0:T(8,128)} fusion(f32[8,1024,1024]{2,1,0:T(8,128)} %get-tuple-element.270, s32[]{:T(128)} %get-tuple-element.269, pred[1024,3072]{1,0:T(32,128)(4,1)S(1)} %bitcast_compare_fusion.2, bf16[3072,1024]{0,1:T(8,128)(2,1)S(1)} %bitcast.48), kind=kOutput, calls=%fused_computation.3.clone.1 | convolution fusion | flops 6442450944 | bytes 13632000 | tf_op jit(solution)/shard_map/while/body/eval_jaxpr/dot_general | solution.py:105
  109.1 0.6 dynamic_slice.20
  109.7 0.6 iota_add_fusion.2
  110.5 3.4 bitcast_compare_fusion.2
  113.9 0.6 broadcast_select_fusion.2
  114.4 8.3 %bitcast_dynamic-update-slice_fusion.2 = f32[8,1024,1024]{2,1,0:T(8,128)} fusion(f32[8,1024,1024]{2,1,0:T(8,128)} %get-tuple-element.270, s32[]{:T(128)} %get-tuple-element.269, pred[1024,3072]{1,0:T(32,128)(4,1)S(1)} %bitcast_compare_fusion.2, bf16[3072,1024]{0,1:T(8,128)(2,1)S(1)} %bitcast.48), kind=kOutput, calls=%fused_computation.3.clone.1 | convolution fusion | flops 6442450944 | bytes 13632000 | tf_op jit(solution)/shard_map/while/body/eval_jaxpr/dot_general | solution.py:105
  122.8 0.6 dynamic_slice.20
  123.4 0.6 iota_add_fusion.2
  124.1 3.4 bitcast_compare_fusion.2
  127.5 0.6 broadcast_select_fusion.2
  128.1 8.3 %bitcast_dynamic-update-slice_fusion.2 = f32[8,1024,1024]{2,1,0:T(8,128)} fusion(f32[8,1024,1024]{2,1,0:T(8,128)} %get-tuple-element.270, s32[]{:T(128)} %get-tuple-element.269, pred[1024,3072]{1,0:T(32,128)(4,1)S(1)} %bitcast_compare_fusion.2, bf16[3072,1024]{0,1:T(8,128)(2,1)S(1)} %bitcast.48), kind=kOutput, calls=%fused_computation.3.clone.1 | convolution fusion | flops 6442450944 | bytes 13632000 | tf_op jit(solution)/shard_map/while/body/eval_jaxpr/dot_general | solution.py:105
  136.4 0.6 dynamic_slice.20
  136.9 0.6 iota_add_fusion.2
  137.7 3.4 bitcast_compare_fusion.2
  141.1 0.6 broadcast_select_fusion.2
  141.6 8.3 %bitcast_dynamic-update-slice_fusion.2 = f32[8,1024,1024]{2,1,0:T(8,128)} fusion(f32[8,1024,1024]{2,1,0:T(8,128)} %get-tuple-element.270, s32[]{:T(128)} %get-tuple-element.269, pred[1024,3072]{1,0:T(32,128)(4,1)S(1)} %bitcast_compare_fusion.2, bf16[3072,1024]{0,1:T(8,128)(2,1)S(1)} %bitcast.48), kind=kOutput, calls=%fused_computation.3.clone.1 | convolution fusion | flops 6442450944 | bytes 13632000 | tf_op jit(solution)/shard_map/while/body/eval_jaxpr/dot_general | solution.py:105
  150.5 0.6 iota_add_fusion.2
  151.2 3.4 bitcast_compare_fusion.2
  154.6 0.6 broadcast_select_fusion.2
  155.2 8.3 %bitcast_dynamic-update-slice_fusion.2 = f32[8,1024,1024]{2,1,0:T(8,128)} fusion(f32[8,1024,1024]{2,1,0:T(8,128)} %get-tuple-element.270, s32[]{:T(128)} %get-tuple-element.269, pred[1024,3072]{1,0:T(32,128)(4,1)S(1)} %bitcast_compare_fusion.2, bf16[3072,1024]{0,1:T(8,128)(2,1)S(1)} %bitcast.48), kind=kOutput, calls=%fused_computation.3.clone.1 | convolution fusion | flops 6442450944 | bytes 13632000 | tf_op jit(solution)/shard_map/while/body/eval_jaxpr/dot_general | solution.py:105
  163.5 31.1 %copy.51 = f32[8192,1024]{0,1:T(8,128)} copy(f32[8192,1024]{1,0:T(8,128)} %bitcast.49) | data formatting | bytes 67108864 | tf_op jit(solution)/shard_map/reshape | solution.py:109
  194.9 229.4 %reduce-scatter.2.cloned.1.call-done = f32[2048,1024]{0,1:T(8,128)} async-done(((f32[8192,1024]{0,1:T(8,128)}), f32[2048,1024]{0,1:T(8,128)}) %reduce-scatter.2.cloned.1.call-update) | async-done | bytes 8388624 | tf_op jit(solution)/shard_map/reduce_scatter | solution.py:108
  424.3 8.6 %copy.62 = f32[128,8,16,128]{3,2,1,0:T(8,128)} copy(f32[128,8,16,128]{3,1,2,0:T(8,128)} %bitcast.51) | data formatting | bytes 16777216
  432.8 15.0 %fusion.2 = f32[16,128,16,64]{1,2,3,0:T(8,128)} fusion(f32[16,128,16,64]{1,0,3,2:T(8,128)} %bitcast.50), kind=kOutput, calls=%fused_computation.8 | output fusion | flops 31457280 | bytes 16777216 | tf_op jit(solution)/shard_map/jit(cumsum)/reduce_window_sum | solution.py:112
  447.8 1.1 slice.20
  448.9 1.0 copy.53
  450.2 39.9 %psum.15 = f32[16,64]{1,0:T(8,128)S(1)} all-reduce(f32[16,64]{1,0:T(8,128)S(1)} %fusion.5), channel_id=1, replica_groups=mesh['rows'=4,'feat'=8] {'rows','feat'}, use_global_device_ids=true, to_apply=%region_13.14 | all-reduce | flops 1024 | bytes 8192 | tf_op jit(solution)/shard_map/psum | solution.py:90
  490.7 5.8 %while.26 = (s32[]{:T(128)}, f32[128,16,64]{2,1,0:T(8,128)S(1)}, s32[]{:T(128)}, f32[4,128,16,64]{1,3,2,0:T(8,128)}, s32[]{:T(128)}, /*index=5*/s32[]{:T(128)}) while((s32[]{:T(128)}, f32[128,16,64]{2,1,0:T(8,128)S(1)}, s32[]{:T(128)}, f32[4,128,16,64]{1,3,2,0:T(8,128)}, s32[]{:T(128)}, /*index=5*/s32[]{:T(128)}) %tuple.67), condition=%wide.region_12.13_spmd.clone, body=%wide.region_11.12_spmd.clone.sunk | while | flops 393220 | bytes 3670109 | solution.py:31
  490.7 1.1 constant_dynamic-slice_fusion.2
  492.6 1.1 constant_dynamic-slice_fusion.2
  494.5 1.1 constant_dynamic-slice_fusion.2
  497.0 4.4 broadcast_add_fusion
  501.4 2.7 subtract_reduce_fusion
  504.2 8.0 %all_to_all.18 = f32[16,128,16]{1,2,0:T(8,128)S(1)} all-to-all(f32[16,128,16]{1,2,0:T(8,128)S(1)} %copy.59), channel_id=1, replica_groups=mesh['rows'=4,'feat'=8] {'rows'}, dimensions={0} | all-to-all | bytes 262144 | tf_op jit(solution)/shard_map/all_to_all | solution.py:117
  512.2 0.7 copy.60
  (50 shorter events, 6.1 us)
Async XLA Ops:
  7.2 26.9 %copy-start = (f32[16,32]{1,0:T(8,128)S(1)}, f32[16,32]{1,0:T(8,128)}, u32[]{:S(2)}) copy-start(f32[16,32]{1,0:T(8,128)} %param.17) | copy-start | bytes 6148
  7.2 417.1 %reduce-scatter.2.cloned.1.call-start = ((), (), s32[]{:S(2)}) async-start(), calls=%async_computation.2 | async-start | bytes 41943040 | tf_op jit(solution)/shard_map/reduce_scatter | solution.py:108
  36.0 4.2 collective-permute-start
  40.2 6.7 %collective-permute-start.1 = (bf16[768,64]{0,1:T(8,128)(2,1)S(1)}, bf16[768,64]{0,1:T(8,128)(2,1)S(1)}, u32[]{:S(2)}, u32[]{:S(2)}) collective-permute-start(bf16[768,64]{0,1:T(8,128)(2,1)S(1)} %maximum_select_fusion.2), channel_id=1, source_target_pairs={{0,2},{1,3},{2,0},{3,1},{4,6},{5,7},{6,4},{7,5},{8,10},{9,11},{10,... | collective-permute-start | bytes 294920 | tf_op jit(solution)/shard_map/ppermute | solution.py:14
  46.9 7.8 %collective-permute-start.2 = (bf16[1536,64]{0,1:T(8,128)(2,1)S(1)}, bf16[1536,64]{0,1:T(8,128)(2,1)S(1)}, u32[]{:S(2)}, u32[]{:S(2)}) collective-permute-start(bf16[1536,64]{0,1:T(8,128)(2,1)S(1)} %maximum_select_fusion.1), channel_id=1, source_target_pairs={{0,4},{1,5},{2,6},{3,7},{4,0},{5,1},{6,2},{7,3},{8,12},{9,13},{10,... | collective-permute-start | bytes 589832 | tf_op jit(solution)/shard_map/ppermute | solution.py:14
  194.6 295.8 %all-gather.2.cloned.1.call-start = ((), (), s32[]{:S(2)}) async-start(), calls=%async_computation.3 | async-start | bytes 2621440 | tf_op jit(solution)/shard_map/all_gather | solution.py:24
  490.1 0.6 copy-start.2
  497.0 15.9 %copy-start.1 = (f32[16,32]{1,0:T(8,128)S(1)}, f32[16,32]{1,0:T(8,128)}, u32[]{:S(2)}) copy-start(f32[16,32]{1,0:T(8,128)} %param.17) | copy-start | bytes 6148
Sparse Core Ops, SparseCore 0:
  194.7 229.4 reduce-scatter.1
  450.1 22.7 all-gather.1
